TPU v7x, 32 devices: a whole 2x2x4 slice. The times are simulated.
32 devices in a mesh: gx: 4 (over y, core), gz: 4 (over z), grp: 2 (over x).
Axes of the slice: x: 2, y: 2, z: 4, core: 2. Of those that a mesh axis runs over, the one named last changes fastest.
Arguments:
- velocity: float32 [3, 3, 512, 2048], P(None, None, ('gz', 'grp'), 'gx'), may hold values from -5 to 5
- slab_average_downflow_speed: float32 [3], replicated, may hold values from 0.5 to 2
- mean_shear: float32 [3], replicated, may hold values from -2 to 2
- mode_counts: int32 [3, 2], replicated, may hold values from 64 to 128
Outputs:
- advanced: float32 [3, 3, 512, 2048], P(None, None, ('gz', 'grp'), 'gx')
- stress: float32 [6, 3, 512, 2048], P(None, None, ('gz', 'grp'), 'gx')
All inputs are finite; a program needn't handle non-finite values.
Results may differ from a plain program's by a relative error of at most 0.00015.
Values sent between devices are 32-bit elements; how exact they have to be, the bound alone decides.
A program may use at most 64 MiB of HBM per device.

v0:
```python
import math
import jax
import jax.numpy as jnp
from jax import lax
from jax.sharding import PartitionSpec as P

NX = 2048
NZ = 512
MODES = 256
molecular_diffusivity = 0.4
time_step = 0.2
highest = lax.Precision.HIGHEST
pair_first = (0, 0, 0, 1, 1, 2)
pair_second = (0, 1, 2, 1, 2, 2)


def with_halo(cells, sides, width):
    for axis, dim in sides:
        count = lax.axis_size(axis)
        head = lax.slice_in_dim(cells, 0, width, axis=dim)
        tail = lax.slice_in_dim(cells, cells.shape[dim] - width, cells.shape[dim], axis=dim)
        cells = jnp.concatenate(
            [
                lax.ppermute(tail, axis, [(i, (i + 1) % count) for i in range(count)]),
                cells,
                lax.ppermute(head, axis, [((i + 1) % count, i) for i in range(count)]),
            ],
            axis=dim,
        )
    return cells


def wave_numbers(modes):
    column = jnp.arange(modes, dtype=jnp.int32)
    half_modes = modes // 2
    return jnp.where(column < half_modes, column, column - half_modes + 1)


def wave_table(positions, length, modes):
    column = jnp.arange(modes, dtype=jnp.int32)
    numbers = wave_numbers(modes)
    phase_int = positions[:, None] * numbers[None, :] % length
    angles = phase_int.astype(jnp.float32) * jnp.float32(2.0 * math.pi / length)
    return jnp.where(column[None, :] < modes // 2, jnp.cos(angles), jnp.sin(angles))


def mode_weights(length, modes):
    column = jnp.arange(modes, dtype=jnp.int32)
    return jnp.where(column == 0, jnp.float32(1.0 / length), jnp.float32(2.0 / length))


def tendency_from(
    middle_entry,
    east_cells,
    west_cells,
    north_cells,
    south_cells,
    slab_average_downflow_speed,
    mean_shear,
):
    downflow_derivative_field = (east_cells - west_cells) * 0.5
    crossflow_derivative_field = (north_cells - south_cells) * 0.5
    diffusion_contribution = (
        east_cells + west_cells + north_cells + south_cells - 4.0 * middle_entry
    )
    holding_slab = slab_average_downflow_speed[:, None, None] + middle_entry[0]
    advanced_state = (
        -holding_slab[None] * downflow_derivative_field
        - middle_entry[2][None] * crossflow_derivative_field
        + molecular_diffusivity * diffusion_contribution
    )
    shear_term = mean_shear[:, None, None] * middle_entry[1]
    return jnp.concatenate([advanced_state[0:1] - shear_term[None], advanced_state[1:]], axis=0)


def runge_kutta(velocity, rate):
    first = velocity + time_step * rate(velocity)
    second = 0.75 * velocity + 0.25 * (first + time_step * rate(first))
    return velocity / 3.0 + 2.0 / 3.0 * (second + time_step * rate(second))


def with_products(components):
    products = [
        components[first_idx] * components[second_idx]
        for first_idx, second_idx in zip(pair_first, pair_second)
    ]
    return jnp.concatenate([components, jnp.stack(products)], axis=0)


def padded_rate(padded, slab_average_downflow_speed, mean_shear):
    return tendency_from(
        padded[:, :, 1:-1, 1:-1],
        padded[:, :, 1:-1, 2:],
        padded[:, :, 1:-1, :-2],
        padded[:, :, 2:, 1:-1],
        padded[:, :, :-2, 1:-1],
        slab_average_downflow_speed,
        mean_shear,
    )


def local(velocity, slab_average_downflow_speed, mean_shear, mode_counts):
    plane_count = velocity.shape[1]
    cells_z = velocity.shape[2]
    cells_x = velocity.shape[3]

    def rate(field):
        padded = with_halo(field, ((("gz", "grp"), 2), ("gx", 3)), 1)
        return padded_rate(padded, slab_average_downflow_speed, mean_shear)

    advanced = runge_kutta(velocity, rate)
    streamwise_devices = lax.axis_size("gx")
    spanwise_devices = lax.axis_size(("gz", "grp"))
    modes_x_local = MODES // streamwise_devices
    modes_z_local = MODES // spanwise_devices
    x_positions = lax.axis_index("gx") * cells_x + jnp.arange(cells_x, dtype=jnp.int32)
    z_positions = lax.axis_index(("gz", "grp")) * cells_z + jnp.arange(cells_z, dtype=jnp.int32)
    synth_x = wave_table(x_positions, NX, MODES)
    synth_z = wave_table(z_positions, NZ, MODES)
    tile_fields = with_products(advanced)
    analysis_x = synth_x * mode_weights(NX, MODES)[None, :]
    columns = analysis_x
    streamwise = lax.psum_scatter(
        jnp.einsum("fpzx,xm->mfpz", tile_fields, columns, precision=highest),
        "gx",
        scatter_dimension=0,
        tiled=True,
    )
    line_count = modes_x_local * 9 * plane_count
    per_device = -(-line_count // spanwise_devices)
    padded_count = per_device * spanwise_devices
    flat_lines = streamwise.reshape(line_count, cells_z)
    flat_lines = jnp.pad(flat_lines, ((0, padded_count - line_count), (0, 0)))
    zlines = lax.all_to_all(flat_lines, ("gz", "grp"), split_axis=0, concat_axis=1, tiled=True)
    whole_z = (
        wave_table(jnp.arange(NZ, dtype=jnp.int32), NZ, MODES) * mode_weights(NZ, MODES)[None, :]
    )
    zcoeffs = jnp.einsum("iz,zn->ni", zlines, whole_z, precision=highest)
    gathered = lax.all_to_all(zcoeffs, ("gz", "grp"), split_axis=0, concat_axis=1, tiled=True)
    spectral = gathered[:, :line_count].reshape(modes_z_local, modes_x_local, 9, plane_count)
    numbers = wave_numbers(MODES)
    z_modes = lax.axis_index(("gz", "grp")) * modes_z_local + jnp.arange(
        modes_z_local, dtype=jnp.int32
    )
    x_modes = lax.axis_index("gx") * modes_x_local + jnp.arange(modes_x_local, dtype=jnp.int32)
    keep_z = jnp.take(numbers, z_modes)[:, None] <= mode_counts[:, 1][None, :]
    keep_x = jnp.take(numbers, x_modes)[:, None] <= mode_counts[:, 0][None, :]
    keep = (keep_z[:, None, :] & keep_x[None, :, :]).astype(jnp.float32)
    spectral = spectral * keep[:, :, None, :]
    columns = synth_z
    partial_sum = jnp.einsum(
        "nmfp,zn->mfpz",
        lax.all_gather(spectral, ("gz", "grp"), axis=0, tiled=True),
        columns,
        precision=highest,
    )
    columns = synth_x
    filtered = jnp.einsum(
        "mfpz,xm->fpzx",
        lax.all_gather(partial_sum, "gx", axis=0, tiled=True),
        columns,
        precision=highest,
    )
    stresses = [
        filtered[3 + index] - filtered[first_idx] * filtered[second_idx]
        for index, (first_idx, second_idx) in enumerate(zip(pair_first, pair_second))
    ]
    return (advanced, jnp.stack(stresses))


def solution(mesh):
    return jax.shard_map(
        local,
        mesh=mesh,
        in_specs=(P(None, None, ("gz", "grp"), "gx"), P(), P(), P()),
        out_specs=(P(None, None, ("gz", "grp"), "gx"), P(None, None, ("gz", "grp"), "gx")),
        check_vma=False,
    )
```

profile of v0, /device:TPU:0, one launch (start us, length us, event | category | flops | bytes accessed | tf_op | source)
XLA Modules:
  0.0 298.7 jit_solution(3138307370650989517)
XLA Ops:
  7.2 1.1 fusion.98
  8.3 3.0 %collective-permute-start = (f32[3,3,1,512]{3,2,1,0:T(1,128)S(1)}, f32[3,3,1,512]{3,2,1,0:T(1,128)S(1)}, u32[]{:S(2)}, u32[]{:S(2)}) collective-permute-start(f32[3,3,1,512]{3,2,1,0:T(1,128)S(1)} %get-tuple-element.20), channel_id=1, source_target_pairs={{0,1},{1,2},{2,3},{3,4},{4,5},{5,6},{6,7},{7,0},{8,9},{9,10},{10,1... | collective-permute-start | bytes 55304 | tf_op jit(solution)/shard_map/ppermute | solution.py:24
  11.3 3.1 %collective-permute-start.1 = (f32[3,3,1,512]{3,2,1,0:T(1,128)S(1)}, f32[3,3,1,512]{3,2,1,0:T(1,128)S(1)}, u32[]{:S(2)}, u32[]{:S(2)}) collective-permute-start(f32[3,3,1,512]{3,2,1,0:T(1,128)S(1)} %get-tuple-element.21), channel_id=1, source_target_pairs={{1,0},{2,1},{3,2},{4,3},{5,4},{6,5},{7,6},{0,7},{9,8},{10,9},{11,1... | collective-permute-start | bytes 55304 | tf_op jit(solution)/shard_map/ppermute | solution.py:26
  14.4 1.2 multiply_bitcast_fusion.1
  15.7 0.4 collective-permute-done
  16.4 1.7 collective-permute-start.2
  18.1 6.3 %collective-permute-done.3 = f32[3,3,66,1]{3,2,1,0:T(8,128)S(1)} collective-permute-done((f32[3,3,66,1]{3,2,1,0:T(8,128)S(1)}, f32[3,3,66,1]{3,2,1,0:T(8,128)S(1)}, u32[]{:S(2)}, u32[]{:S(2)}) %collective-permute-start.3) | collective-permute-done | bytes 2408 | tf_op jit(solution)/shard_map/ppermute | solution.py:24
  24.5 1.2 collective-permute-done.2
  25.7 1.2 multiply_add_fusion.2
  27.0 0.6 copy-done.4
  28.0 1.3 collective-permute-start.4
  29.3 3.5 %collective-permute-start.5 = (f32[3,3,1,512]{3,2,1,0:T(1,128)S(1)}, f32[3,3,1,512]{3,2,1,0:T(1,128)S(1)}, u32[]{:S(2)}, u32[]{:S(2)}) collective-permute-start(f32[3,3,1,512]{3,2,1,0:T(1,128)S(1)} %get-tuple-element.17), channel_id=1, source_target_pairs={{1,0},{2,1},{3,2},{4,3},{5,4},{6,5},{7,6},{0,7},{9,8},{10,9},{11,1... | collective-permute-start | bytes 55304 | tf_op jit(solution)/shard_map/ppermute | solution.py:26
  32.8 1.8 collective-permute-done.4
  35.0 1.7 collective-permute-start.6
  36.7 6.2 %collective-permute-done.7 = f32[3,3,66,1]{3,2,1,0:T(8,128)S(1)} collective-permute-done((f32[3,3,66,1]{3,2,1,0:T(8,128)S(1)}, f32[3,3,66,1]{3,2,1,0:T(8,128)S(1)}, u32[]{:S(2)}, u32[]{:S(2)}) %collective-permute-start.7) | collective-permute-done | bytes 2408 | tf_op jit(solution)/shard_map/ppermute | solution.py:24
  43.0 1.2 collective-permute-done.6
  44.2 1.2 multiply_add_fusion.1
  45.6 0.4 fusion.5
  46.1 4.8 %collective-permute-start.9 = (f32[3,3,1,512]{3,2,1,0:T(1,128)S(1)}, f32[3,3,1,512]{3,2,1,0:T(1,128)S(1)}, u32[]{:S(2)}, u32[]{:S(2)}) collective-permute-start(f32[3,3,1,512]{3,2,1,0:T(1,128)S(1)} %get-tuple-element.13), channel_id=1, source_target_pairs={{1,0},{2,1},{3,2},{4,3},{5,4},{6,5},{7,6},{0,7},{9,8},{10,9},{11,1... | collective-permute-start | bytes 55304 | tf_op jit(solution)/shard_map/ppermute | solution.py:26
  50.9 1.7 collective-permute-done.8
  52.8 1.9 collective-permute-start.10
  54.8 5.7 %collective-permute-done.11 = f32[3,3,66,1]{3,2,1,0:T(8,128)S(1)} collective-permute-done((f32[3,3,66,1]{3,2,1,0:T(8,128)S(1)}, f32[3,3,66,1]{3,2,1,0:T(8,128)S(1)}, u32[]{:S(2)}, u32[]{:S(2)}) %collective-permute-start.11) | collective-permute-done | bytes 2408 | tf_op jit(solution)/shard_map/ppermute | solution.py:24
  60.5 1.9 collective-permute-done.10
  62.4 1.2 multiply_add_fusion
  63.8 0.4 constant_dynamic-update-slice_fusion
  64.5 0.7 copy-done.1
  65.3 15.6 %fusion.16 = f32[256,9,3,64]{3,0,2,1:T(8,128)} fusion(f32[9,3,64,512]{3,2,1,0:T(8,128)S(1)} %multiply_dynamic-update-slice_fusion, f32[256]{0:T(256)S(1)} %compare_select_fusion.4, s32[256]{0:T(256)S(1)} %add_select_fusion.4, s32[512]{0:T(512)S(1)} %iota_add_fusion, pred[256]{0:T(512)(128)(4,1)S(1)} %iota_compare_fusion), kind=kOutput, calls=%fused_computation.57 | convolution fusion | flops 2720006144 | bytes 5312768 | tf_op jit(solution)/shard_map/fpzx,xm->mfpz/dot_general | solution.py:124
  81.0 0.8 gather_fusion.1
  81.7 0.7 gather_fusion
  82.5 40.7 %reduce-scatter.2.cloned.1.call-done = f32[64,9,3,64]{3,0,2,1:T(8,128)} async-done(((f32[256,9,3,64]{3,0,2,1:T(8,128)}), f32[64,9,3,64]{3,0,2,1:T(8,128)}) %reduce-scatter.2.cloned.1.call-update) | async-done | bytes 442384 | tf_op jit(solution)/shard_map/reduce_scatter | solution.py:123
  123.2 1.8 copy.13
  125.0 0.4 all_to_all.24
  125.4 1.1 copy.14
  126.5 5.5 %all-to-all-start = ((f32[8,216,64]{1,2,0:T(8,128)}), f32[8,216,64]{1,2,0:T(8,128)S(1)}, u32[]{:S(2)}, u32[]{:S(2)}) async-start(f32[8,216,64]{1,2,0:T(8,128)} %copy.14), calls=%async_computation.1 | async-start | bytes 1048576 | tf_op jit(solution)/shard_map/all_to_all | solution.py:134
  132.2 14.2 %all-to-all-done = f32[8,216,64]{1,2,0:T(8,128)S(1)} async-done(((f32[8,216,64]{1,2,0:T(8,128)}), f32[8,216,64]{1,2,0:T(8,128)S(1)}, u32[]{:S(2)}, u32[]{:S(2)}) %all-to-all-start) | async-done | bytes 442400 | tf_op jit(solution)/shard_map/all_to_all | solution.py:134
  146.4 4.6 %fusion.18 = f32[8,32,216]{2,1,0:T(8,128)} fusion(f32[216,512,1]{0,1,2:T(8,128)S(1)} %bitcast.48, f32[8,32]{1,0:T(8,128)S(1)} %fusion.76, s32[8,32]{1,0:T(8,128)S(1)} %add_select_fusion.3, pred[8,32]{1,0:T(8,128)(4,1)S(1)} %fusion.75), kind=kOutput, calls=%fused_computation.59 | convolution fusion | flops 341835776 | bytes 665856 | tf_op jit(solution)/shard_map/iz,zn->ni/dot_general | solution.py:138
  151.0 3.6 %all-to-all-start.1 = ((f32[8,32,216]{2,1,0:T(8,128)}), f32[8,32,216]{2,1,0:T(8,128)S(1)}, u32[]{:S(2)}, u32[]{:S(2)}) async-start(f32[8,32,216]{2,1,0:T(8,128)} %fusion.18), calls=%async_computation.2 | async-start | bytes 524288 | tf_op jit(solution)/shard_map/all_to_all | solution.py:139
  154.9 8.7 %all-to-all-done.1 = f32[8,32,216]{2,1,0:T(8,128)S(1)} async-done(((f32[8,32,216]{2,1,0:T(8,128)}), f32[8,32,216]{2,1,0:T(8,128)S(1)}, u32[]{:S(2)}, u32[]{:S(2)}) %all-to-all-start.1) | async-done | bytes 221216 | tf_op jit(solution)/shard_map/all_to_all | solution.py:139
  163.7 0.3 copy.16
  164.0 0.4 reshape.244
  164.6 1.1 copy.17
  165.7 0.4 all-gather.5.cloned.1.call-start
  166.2 62.4 %all-gather.3.cloned.1.call-done = f32[256,64,9,3]{1,0,3,2:T(8,128)} async-done(((f32[32,64,9,3]{1,0,3,2:T(8,128)}), f32[256,64,9,3]{1,0,3,2:T(8,128)}) %all-gather.3.cloned.1.call-update) | async-done | bytes 1769488 | tf_op jit(solution)/shard_map/all_gather | solution.py:153
  228.6 7.8 %fusion.58 = f32[64,9,3,64]{3,0,2,1:T(8,128)S(1)} fusion(f32[256,64,9,3]{1,0,3,2:T(8,128)} %all-gather.3.cloned.1.call-done, s32[256]{0:T(256)S(1)} %add_select_fusion.4, s32[64]{0:T(128)S(1)} %iota_add_fusion.1, pred[256]{0:T(512)(128)(4,1)S(1)} %iota_compare_fusion), kind=kOutput, calls=%fused_computation.133 | convolution fusion | flops 339984384 | bytes 2213376 | tf_op jit(solution)/shard_map/nmfp,zn->mfpz/dot_general | solution.py:151
  236.4 1.6 copy.18
  238.0 36.3 %all-gather.5.cloned.1.call-done = f32[256,9,3,64]{3,2,1,0:T(4,128)} async-done(((f32[64,9,3,64]{3,2,1,0:T(4,128)}), f32[256,9,3,64]{3,2,1,0:T(4,128)}) %all-gather.5.cloned.1.call-update) | async-done | bytes 1769488 | tf_op jit(solution)/shard_map/all_gather | solution.py:160
  274.4 15.7 %fusion = f32[9,3,64,512]{3,2,1,0:T(8,128)S(1)} fusion(f32[256,9,3,64]{3,2,1,0:T(4,128)} %all-gather.5.cloned.1.call-done, s32[256]{0:T(256)S(1)} %add_select_fusion.4, s32[512]{0:T(512)S(1)} %iota_add_fusion, pred[256]{0:T(512)(128)(4,1)S(1)} %iota_compare_fusion), kind=kOutput, calls=%fused_computation.2 | convolution fusion | flops 2719875072 | bytes 5311744 | tf_op jit(solution)/shard_map/mfpz,xm->fpzx/dot_general | solution.py:158
  290.6 1.4 copy-done.2
  (65 shorter events, 3.4 us)
Async XLA Ops:
  7.2 9.0 %copy-start = (f32[3,3,64,512]{3,2,1,0:T(8,128)S(1)}, f32[3,3,64,512]{3,2,1,0:T(8,128)}, u32[]{:S(2)}) copy-start(f32[3,3,64,512]{3,2,1,0:T(8,128)} %param.4) | copy-start | bytes 3538948
  7.2 116.1 %reduce-scatter.2.cloned.1.call-start = ((), (), s32[]{:S(2)}) async-start(), calls=%async_computation.3 | async-start | bytes 4423680 | tf_op jit(solution)/shard_map/reduce_scatter | solution.py:123
  8.3 7.8 %collective-permute-start = (f32[3,3,1,512]{3,2,1,0:T(1,128)S(1)}, f32[3,3,1,512]{3,2,1,0:T(1,128)S(1)}, u32[]{:S(2)}, u32[]{:S(2)}) collective-permute-start(f32[3,3,1,512]{3,2,1,0:T(1,128)S(1)} %get-tuple-element.20), channel_id=1, source_target_pairs={{0,1},{1,2},{2,3},{3,4},{4,5},{5,6},{6,7},{7,0},{8,9},{9,10},{10,1... | collective-permute-start | bytes 55304 | tf_op jit(solution)/shard_map/ppermute | solution.py:24
  11.3 4.8 %collective-permute-start.1 = (f32[3,3,1,512]{3,2,1,0:T(1,128)S(1)}, f32[3,3,1,512]{3,2,1,0:T(1,128)S(1)}, u32[]{:S(2)}, u32[]{:S(2)}) collective-permute-start(f32[3,3,1,512]{3,2,1,0:T(1,128)S(1)} %get-tuple-element.21), channel_id=1, source_target_pairs={{1,0},{2,1},{3,2},{4,3},{5,4},{6,5},{7,6},{0,7},{9,8},{10,9},{11,1... | collective-permute-start | bytes 55304 | tf_op jit(solution)/shard_map/ppermute | solution.py:26
  16.3 8.1 %collective-permute-start.3 = (f32[3,3,66,1]{3,2,1,0:T(8,128)S(1)}, f32[3,3,66,1]{3,2,1,0:T(8,128)S(1)}, u32[]{:S(2)}, u32[]{:S(2)}) collective-permute-start(f32[3,3,66,1]{3,2,1,0:T(8,128)S(1)} %get-tuple-element.8), channel_id=1, source_target_pairs={{0,8},{8,16},{16,24},{24,0},{1,9},{9,17},{17,25},{25,1},{2,10},{10... | collective-permute-start | bytes 7136 | tf_op jit(solution)/shard_map/ppermute | solution.py:24
  16.4 9.3 %collective-permute-start.2 = (f32[3,3,66,1]{3,2,1,0:T(8,128)S(1)}, f32[3,3,66,1]{3,2,1,0:T(8,128)S(1)}, u32[]{:S(2)}, u32[]{:S(2)}) collective-permute-start(f32[3,3,66,1]{3,2,1,0:T(8,128)S(1)} %get-tuple-element.9), channel_id=1, source_target_pairs={{8,0},{16,8},{24,16},{0,24},{9,1},{17,9},{25,17},{1,25},{10,2},{18... | collective-permute-start | bytes 7136 | tf_op jit(solution)/shard_map/ppermute | solution.py:26
  26.9 0.7 copy-start.4
  27.9 8.7 %copy-start.3 = (f32[3]{0:T(128)S(1)}, f32[3]{0:T(128)}, u32[]{:S(2)}) copy-start(f32[3]{0:T(128)} %param.5) | copy-start | bytes 40
  28.0 6.7 %collective-permute-start.4 = (f32[3,3,1,512]{3,2,1,0:T(1,128)S(1)}, f32[3,3,1,512]{3,2,1,0:T(1,128)S(1)}, u32[]{:S(2)}, u32[]{:S(2)}) collective-permute-start(f32[3,3,1,512]{3,2,1,0:T(1,128)S(1)} %get-tuple-element.16), channel_id=1, source_target_pairs={{0,1},{1,2},{2,3},{3,4},{4,5},{5,6},{6,7},{7,0},{8,9},{9,10},{10,1... | collective-permute-start | bytes 55304 | tf_op jit(solution)/shard_map/ppermute | solution.py:24
  29.3 5.4 %collective-permute-start.5 = (f32[3,3,1,512]{3,2,1,0:T(1,128)S(1)}, f32[3,3,1,512]{3,2,1,0:T(1,128)S(1)}, u32[]{:S(2)}, u32[]{:S(2)}) collective-permute-start(f32[3,3,1,512]{3,2,1,0:T(1,128)S(1)} %get-tuple-element.17), channel_id=1, source_target_pairs={{1,0},{2,1},{3,2},{4,3},{5,4},{6,5},{7,6},{0,7},{9,8},{10,9},{11,1... | collective-permute-start | bytes 55304 | tf_op jit(solution)/shard_map/ppermute | solution.py:26
  34.8 8.1 %collective-permute-start.7 = (f32[3,3,66,1]{3,2,1,0:T(8,128)S(1)}, f32[3,3,66,1]{3,2,1,0:T(8,128)S(1)}, u32[]{:S(2)}, u32[]{:S(2)}) collective-permute-start(f32[3,3,66,1]{3,2,1,0:T(8,128)S(1)} %get-tuple-element.6), channel_id=1, source_target_pairs={{0,8},{8,16},{16,24},{24,0},{1,9},{9,17},{17,25},{25,1},{2,10},{10... | collective-permute-start | bytes 7136 | tf_op jit(solution)/shard_map/ppermute | solution.py:24
  35.0 9.2 %collective-permute-start.6 = (f32[3,3,66,1]{3,2,1,0:T(8,128)S(1)}, f32[3,3,66,1]{3,2,1,0:T(8,128)S(1)}, u32[]{:S(2)}, u32[]{:S(2)}) collective-permute-start(f32[3,3,66,1]{3,2,1,0:T(8,128)S(1)} %get-tuple-element.7), channel_id=1, source_target_pairs={{8,0},{16,8},{24,16},{0,24},{9,1},{17,9},{25,17},{1,25},{10,2},{18... | collective-permute-start | bytes 7136 | tf_op jit(solution)/shard_map/ppermute | solution.py:26
  46.1 6.5 %collective-permute-start.8 = (f32[3,3,1,512]{3,2,1,0:T(1,128)S(1)}, f32[3,3,1,512]{3,2,1,0:T(1,128)S(1)}, u32[]{:S(2)}, u32[]{:S(2)}) collective-permute-start(f32[3,3,1,512]{3,2,1,0:T(1,128)S(1)} %get-tuple-element.12), channel_id=1, source_target_pairs={{0,1},{1,2},{2,3},{3,4},{4,5},{5,6},{6,7},{7,0},{8,9},{9,10},{10,1... | collective-permute-start | bytes 55304 | tf_op jit(solution)/shard_map/ppermute | solution.py:24
  46.1 6.5 %collective-permute-start.9 = (f32[3,3,1,512]{3,2,1,0:T(1,128)S(1)}, f32[3,3,1,512]{3,2,1,0:T(1,128)S(1)}, u32[]{:S(2)}, u32[]{:S(2)}) collective-permute-start(f32[3,3,1,512]{3,2,1,0:T(1,128)S(1)} %get-tuple-element.13), channel_id=1, source_target_pairs={{1,0},{2,1},{3,2},{4,3},{5,4},{6,5},{7,6},{0,7},{9,8},{10,9},{11,1... | collective-permute-start | bytes 55304 | tf_op jit(solution)/shard_map/ppermute | solution.py:26
  52.8 7.7 %collective-permute-start.11 = (f32[3,3,66,1]{3,2,1,0:T(8,128)S(1)}, f32[3,3,66,1]{3,2,1,0:T(8,128)S(1)}, u32[]{:S(2)}, u32[]{:S(2)}) collective-permute-start(f32[3,3,66,1]{3,2,1,0:T(8,128)S(1)} %get-tuple-element.4), channel_id=1, source_target_pairs={{0,8},{8,16},{16,24},{24,0},{1,9},{9,17},{17,25},{25,1},{2,10},{10... | collective-permute-start | bytes 7136 | tf_op jit(solution)/shard_map/ppermute | solution.py:24
  52.8 9.6 %collective-permute-start.10 = (f32[3,3,66,1]{3,2,1,0:T(8,128)S(1)}, f32[3,3,66,1]{3,2,1,0:T(8,128)S(1)}, u32[]{:S(2)}, u32[]{:S(2)}) collective-permute-start(f32[3,3,66,1]{3,2,1,0:T(8,128)S(1)} %get-tuple-element.5), channel_id=1, source_target_pairs={{8,0},{16,8},{24,16},{0,24},{9,1},{17,9},{25,17},{1,25},{10,2},{18... | collective-permute-start | bytes 7136 | tf_op jit(solution)/shard_map/ppermute | solution.py:26
  64.2 1.0 copy-start.1
  125.4 6.7 %copy-start.5 = (s32[3,2]{0,1:T(2,128)S(1)}, s32[3,2]{0,1:T(2,128)}, u32[]{:S(2)}) copy-start(s32[3,2]{0,1:T(2,128)} %param.7) | copy-start | bytes 76
  126.5 19.8 %all-to-all-start = ((f32[8,216,64]{1,2,0:T(8,128)}), f32[8,216,64]{1,2,0:T(8,128)S(1)}, u32[]{:S(2)}, u32[]{:S(2)}) async-start(f32[8,216,64]{1,2,0:T(8,128)} %copy.14), calls=%async_computation.1 | async-start | bytes 1048576 | tf_op jit(solution)/shard_map/all_to_all | solution.py:134
  151.0 12.6 %all-to-all-start.1 = ((f32[8,32,216]{2,1,0:T(8,128)}), f32[8,32,216]{2,1,0:T(8,128)S(1)}, u32[]{:S(2)}, u32[]{:S(2)}) async-start(f32[8,32,216]{2,1,0:T(8,128)} %fusion.18), calls=%async_computation.2 | async-start | bytes 524288 | tf_op jit(solution)/shard_map/all_to_all | solution.py:139
  154.7 73.9 %all-gather.3.cloned.1.call-start = ((), (), s32[]{:S(2)}) async-start(), calls=%async_computation.4 | async-start | bytes 3981312 | tf_op jit(solution)/shard_map/all_gather | solution.py:153
  165.7 108.7 %all-gather.5.cloned.1.call-start = ((), (), s32[]{:S(2)}) async-start(), calls=%async_computation.5 | async-start | bytes 5898240 | tf_op jit(solution)/shard_map/all_gather | solution.py:160
  290.6 1.4 copy-start.2
Sparse Core Ops, SparseCore 0:
  81.0 42.1 reduce-scatter.1
  165.8 62.6 all-gather.2
  238.2 36.1 all-gather.4
where the time goes:
time: 304 us; the launch traced here: 299 us
  waiting for transfers between devices  189 us (62%)
  matrix products  43.8 us (14%)
  starting transfers between devices  31 us (10%)
  between operations  14.4 us (5%)
  local copies, waits for them, and re-layouts  12.2 us (4%)
  other arithmetic  8.34 us (3%)
    all_gather x1, waiting for transfers between devices, local(): lax.all_gather(spectral, ('gz', 'grp'), axis=0, tiled=True)  62.4 us
    reduce_scatter x1, waiting for transfers between devices, local(): lax.psum_scatter(jnp.einsum('fpzx,xm->mfpz', tile_fields, columns, precis...  40.7 us
    all_gather x1, waiting for transfers between devices, local(): lax.all_gather(partial_sum, 'gx', axis=0, tiled=True)  36.3 us
    ppermute x6, waiting for transfers between devices, with_halo(): lax.ppermute(tail, axis, [(i, (i + 1) % count) for i in range(count)])  22.2 us
    ppermute x6, starting transfers between devices, with_halo(): lax.ppermute(head, axis, [((i + 1) % count, i) for i in range(count)])  16.7 us
    dot_general x1, matrix products, local(): jnp.einsum('mfpz,xm->fpzx', lax.all_gather(partial_sum, 'gx', axis=0, til...  15.7 us
    dot_general x1, matrix products, local(): jnp.einsum('fpzx,xm->mfpz', tile_fields, columns, precision=highest)  15.6 us
    all_to_all x1, waiting for transfers between devices, local(): lax.all_to_all(flat_lines, ('gz', 'grp'), split_axis=0, concat_axis=1, ti...  14.2 us
  transfers between devices with their start and end apart: 17, of which 14 were waited for; matrix products, arithmetic and copies ran while one was open for 1% of the time, Pallas kernels for 0%

commit v1 on v0

--- a/solution.py
+++ b/solution.py
@@ -155,12 +155,21 @@
         precision=highest,
     )
     columns = synth_x
-    filtered = jnp.einsum(
-        "mfpz,xm->fpzx",
-        lax.all_gather(partial_sum, "gx", axis=0, tiled=True),
-        columns,
-        precision=highest,
-    )
+    length_2, position, extent = (lax.axis_size("gx"), lax.axis_index("gx"), partial_sum.shape[0])
+    forward = [(i_2, (i_2 + 1) % length_2) for i_2 in range(length_2)]
+    block, filtered = (partial_sum, None)
+    for step in range(length_2):
+        coming = lax.ppermute(block, "gx", forward) if step < length_2 - 1 else None
+        update = jnp.einsum(
+            "mfpz,xm->fpzx",
+            block,
+            lax.dynamic_slice_in_dim(
+                columns, (position - step) % length_2 * extent, block.shape[0], axis=1
+            ),
+            precision=highest,
+        )
+        filtered = update if filtered is None else filtered + update
+        block = coming
     stresses = [
         filtered[3 + index] - filtered[first_idx] * filtered[second_idx]
         for index, (first_idx, second_idx) in enumerate(zip(pair_first, pair_second))

time: 304 us -> 286 us (0.941)
  waiting for transfers between devices: 189 us -> 179 us
  matrix products: 43.8 us -> 34.7 us
    all_gather x1 -> x0, waiting for transfers between devices: 36.3 us -> none  [local(): lax.all_gather(partial_sum, 'gx', axis=0, tiled=True)]
    ppermute x0 -> x3, waiting for transfers between devices: none -> 26.2 us  [local(): coming = lax.ppermute(block, 'gx', forward) if step < length_2 - 1 else None]
    dot_general x1, matrix products: 15.6 us -> 9.82 us  [local(): jnp.einsum('fpzx,xm->mfpz', tile_fields, columns, precision=highest)]
    dot_general x1 -> x4, matrix products: 15.7 us -> 12.4 us  [local(): jnp.einsum('mfpz,xm->fpzx', block, lax.dynamic_slice_in_dim(columns, (pos...]
  transfers between devices with their start and end apart: 17 -> 19, of which waited for: 14 -> 16; matrix products, arithmetic and copies ran while one was open for 1% -> 5% of each run, Pallas kernels for 0% -> 0%
where the time goes in v1:
time: 286 us; the launch traced here: 281 us
  waiting for transfers between devices  179 us (63%)
  matrix products  34.7 us (12%)
  starting transfers between devices  31.3 us (11%)
  between operations  14.8 us (5%)
  other arithmetic  11 us (4%)
  local copies, waits for them, and re-layouts  9.85 us (3%)
    all_gather x1, waiting for transfers between devices, local(): lax.all_gather(spectral, ('gz', 'grp'), axis=0, tiled=True)  62.8 us
    reduce_scatter x1, waiting for transfers between devices, local(): lax.psum_scatter(jnp.einsum('fpzx,xm->mfpz', tile_fields, columns, precis...  40.7 us
    ppermute x3, waiting for transfers between devices, local(): coming = lax.ppermute(block, 'gx', forward) if step < length_2 - 1 else None  26.2 us
    ppermute x6, waiting for transfers between devices, with_halo(): lax.ppermute(tail, axis, [(i, (i + 1) % count) for i in range(count)])  21.6 us
    ppermute x6, starting transfers between devices, with_halo(): lax.ppermute(head, axis, [((i + 1) % count, i) for i in range(count)])  17 us
    all_to_all x1, waiting for transfers between devices, local(): lax.all_to_all(flat_lines, ('gz', 'grp'), split_axis=0, concat_axis=1, ti...  14.2 us
    dot_general x4, matrix products, local(): jnp.einsum('mfpz,xm->fpzx', block, lax.dynamic_slice_in_dim(columns, (pos...  12.4 us
    dot_general x1, matrix products, local(): jnp.einsum('fpzx,xm->mfpz', tile_fields, columns, precision=highest)  9.82 us
  transfers between devices with their start and end apart: 19, of which 16 were waited for; matrix products, arithmetic and copies ran while one was open for 5% of the time, Pallas kernels for 0%

profile of v1, /device:TPU:0, one launch (start us, length us, event | category | flops | bytes accessed | tf_op | source)
XLA Modules:
  0.0 280.8 jit_solution(13616312574056113416)
XLA Ops:
  7.2 1.1 fusion.106
  8.3 3.0 %collective-permute-start = (f32[3,3,1,512]{3,2,1,0:T(1,128)S(1)}, f32[3,3,1,512]{3,2,1,0:T(1,128)S(1)}, u32[]{:S(2)}, u32[]{:S(2)}) collective-permute-start(f32[3,3,1,512]{3,2,1,0:T(1,128)S(1)} %get-tuple-element.20), channel_id=1, source_target_pairs={{0,1},{1,2},{2,3},{3,4},{4,5},{5,6},{6,7},{7,0},{8,9},{9,10},{10,1... | collective-permute-start | bytes 55304 | tf_op jit(solution)/shard_map/ppermute | solution.py:24
  11.3 3.1 %collective-permute-start.1 = (f32[3,3,1,512]{3,2,1,0:T(1,128)S(1)}, f32[3,3,1,512]{3,2,1,0:T(1,128)S(1)}, u32[]{:S(2)}, u32[]{:S(2)}) collective-permute-start(f32[3,3,1,512]{3,2,1,0:T(1,128)S(1)} %get-tuple-element.21), channel_id=1, source_target_pairs={{1,0},{2,1},{3,2},{4,3},{5,4},{6,5},{7,6},{0,7},{9,8},{10,9},{11,1... | collective-permute-start | bytes 55304 | tf_op jit(solution)/shard_map/ppermute | solution.py:26
  14.4 1.2 multiply_bitcast_fusion.1
  16.4 1.7 collective-permute-start.2
  18.1 6.3 %collective-permute-done.3 = f32[3,3,66,1]{3,2,1,0:T(8,128)S(1)} collective-permute-done((f32[3,3,66,1]{3,2,1,0:T(8,128)S(1)}, f32[3,3,66,1]{3,2,1,0:T(8,128)S(1)}, u32[]{:S(2)}, u32[]{:S(2)}) %collective-permute-start.3) | collective-permute-done | bytes 2408 | tf_op jit(solution)/shard_map/ppermute | solution.py:24
  24.5 1.2 collective-permute-done.2
  25.7 1.2 multiply_add_fusion.2
  27.0 0.6 copy-done.4
  28.0 1.3 collective-permute-start.4
  29.3 3.5 %collective-permute-start.5 = (f32[3,3,1,512]{3,2,1,0:T(1,128)S(1)}, f32[3,3,1,512]{3,2,1,0:T(1,128)S(1)}, u32[]{:S(2)}, u32[]{:S(2)}) collective-permute-start(f32[3,3,1,512]{3,2,1,0:T(1,128)S(1)} %get-tuple-element.17), channel_id=1, source_target_pairs={{1,0},{2,1},{3,2},{4,3},{5,4},{6,5},{7,6},{0,7},{9,8},{10,9},{11,1... | collective-permute-start | bytes 55304 | tf_op jit(solution)/shard_map/ppermute | solution.py:26
  32.8 1.8 collective-permute-done.4
  35.0 1.7 collective-permute-start.6
  36.7 6.2 %collective-permute-done.7 = f32[3,3,66,1]{3,2,1,0:T(8,128)S(1)} collective-permute-done((f32[3,3,66,1]{3,2,1,0:T(8,128)S(1)}, f32[3,3,66,1]{3,2,1,0:T(8,128)S(1)}, u32[]{:S(2)}, u32[]{:S(2)}) %collective-permute-start.7) | collective-permute-done | bytes 2408 | tf_op jit(solution)/shard_map/ppermute | solution.py:24
  43.0 1.2 collective-permute-done.6
  44.2 1.2 multiply_add_fusion.1
  45.6 0.4 fusion.3
  46.1 4.8 %collective-permute-start.9 = (f32[3,3,1,512]{3,2,1,0:T(1,128)S(1)}, f32[3,3,1,512]{3,2,1,0:T(1,128)S(1)}, u32[]{:S(2)}, u32[]{:S(2)}) collective-permute-start(f32[3,3,1,512]{3,2,1,0:T(1,128)S(1)} %get-tuple-element.13), channel_id=1, source_target_pairs={{1,0},{2,1},{3,2},{4,3},{5,4},{6,5},{7,6},{0,7},{9,8},{10,9},{11,1... | collective-permute-start | bytes 55304 | tf_op jit(solution)/shard_map/ppermute | solution.py:26
  50.9 1.7 collective-permute-done.8
  52.8 2.2 collective-permute-start.10
  55.1 5.1 %collective-permute-done.11 = f32[3,3,66,1]{3,2,1,0:T(8,128)S(1)} collective-permute-done((f32[3,3,66,1]{3,2,1,0:T(8,128)S(1)}, f32[3,3,66,1]{3,2,1,0:T(8,128)S(1)}, u32[]{:S(2)}, u32[]{:S(2)}) %collective-permute-start.11) | collective-permute-done | bytes 2408 | tf_op jit(solution)/shard_map/ppermute | solution.py:24
  60.2 2.2 collective-permute-done.10
  62.4 1.2 multiply_add_fusion
  63.8 0.4 constant_dynamic-update-slice_fusion
  64.5 0.7 copy-done.1
  65.3 9.8 %fusion.13 = f32[256,9,3,64]{3,0,2,1:T(8,128)} fusion(f32[9,3,64,512]{3,2,1,0:T(8,128)S(1)} %multiply_dynamic-update-slice_fusion, f32[256]{0:T(256)S(1)} %compare_select_fusion.4, s32[256]{0:T(256)S(1)} %add_select_fusion.4, s32[512]{0:T(512)S(1)} %iota_add_fusion, pred[256]{0:T(512)(128)(4,1)S(1)} %iota_compare_fusion), kind=kOutput, calls=%fused_computation.54 | convolution fusion | flops 2720006144 | bytes 5312768 | tf_op jit(solution)/shard_map/fpzx,xm->mfpz/dot_general | solution.py:124
  75.2 0.8 gather_fusion.1
  76.0 0.7 gather_fusion
  76.7 40.7 %reduce-scatter.2.cloned.1.call-done = f32[64,9,3,64]{3,0,2,1:T(8,128)} async-done(((f32[256,9,3,64]{3,0,2,1:T(8,128)}), f32[64,9,3,64]{3,0,2,1:T(8,128)}) %reduce-scatter.2.cloned.1.call-update) | async-done | bytes 442384 | tf_op jit(solution)/shard_map/reduce_scatter | solution.py:123
  117.4 1.8 copy.19
  119.6 1.1 copy.20
  120.8 5.7 %all-to-all-start = ((f32[8,216,64]{1,2,0:T(8,128)}), f32[8,216,64]{1,2,0:T(8,128)S(1)}, u32[]{:S(2)}, u32[]{:S(2)}) async-start(f32[8,216,64]{1,2,0:T(8,128)} %copy.20), calls=%async_computation.1 | async-start | bytes 1048576 | tf_op jit(solution)/shard_map/all_to_all | solution.py:134
  126.6 14.2 %all-to-all-done = f32[8,216,64]{1,2,0:T(8,128)S(1)} async-done(((f32[8,216,64]{1,2,0:T(8,128)}), f32[8,216,64]{1,2,0:T(8,128)S(1)}, u32[]{:S(2)}, u32[]{:S(2)}) %all-to-all-start) | async-done | bytes 442400 | tf_op jit(solution)/shard_map/all_to_all | solution.py:134
  140.8 4.6 %fusion.15 = f32[8,32,216]{2,1,0:T(8,128)} fusion(f32[216,512,1]{0,1,2:T(8,128)S(1)} %bitcast.69, f32[8,32]{1,0:T(8,128)S(1)} %fusion.84, s32[8,32]{1,0:T(8,128)S(1)} %add_select_fusion.3, pred[8,32]{1,0:T(8,128)(4,1)S(1)} %fusion.83), kind=kOutput, calls=%fused_computation.56 | convolution fusion | flops 341835776 | bytes 665856 | tf_op jit(solution)/shard_map/iz,zn->ni/dot_general | solution.py:138
  145.4 3.6 %all-to-all-start.1 = ((f32[8,32,216]{2,1,0:T(8,128)}), f32[8,32,216]{2,1,0:T(8,128)S(1)}, u32[]{:S(2)}, u32[]{:S(2)}) async-start(f32[8,32,216]{2,1,0:T(8,128)} %fusion.15), calls=%async_computation.2 | async-start | bytes 524288 | tf_op jit(solution)/shard_map/all_to_all | solution.py:139
  149.2 8.8 %all-to-all-done.1 = f32[8,32,216]{2,1,0:T(8,128)S(1)} async-done(((f32[8,32,216]{2,1,0:T(8,128)}), f32[8,32,216]{2,1,0:T(8,128)S(1)}, u32[]{:S(2)}, u32[]{:S(2)}) %all-to-all-start.1) | async-done | bytes 221216 | tf_op jit(solution)/shard_map/all_to_all | solution.py:139
  159.1 0.8 broadcast_multiply_fusion
  159.9 62.8 %all-gather.2.cloned.1.call-done = f32[256,64,9,3]{1,0,3,2:T(8,128)} async-done(((f32[32,64,9,3]{1,0,3,2:T(8,128)}), f32[256,64,9,3]{1,0,3,2:T(8,128)}) %all-gather.2.cloned.1.call-update) | async-done | bytes 1769488 | tf_op jit(solution)/shard_map/all_gather | solution.py:153
  222.7 7.9 %fusion.66 = f32[64,9,3,64]{3,0,2,1:T(8,128)S(1)} fusion(f32[256,64,9,3]{1,0,3,2:T(8,128)} %all-gather.2.cloned.1.call-done, s32[256]{0:T(256)S(1)} %add_select_fusion.4, s32[64]{0:T(128)S(1)} %iota_add_fusion.1, pred[256]{0:T(512)(128)(4,1)S(1)} %iota_compare_fusion), kind=kOutput, calls=%fused_computation.141 | convolution fusion | flops 339984384 | bytes 2213376 | tf_op jit(solution)/shard_map/nmfp,zn->mfpz/dot_general | solution.py:151
  230.7 12.5 %collective-permute-done.12 = f32[64,9,3,64]{3,0,2,1:T(8,128)S(1)} collective-permute-done((f32[64,9,3,64]{3,0,2,1:T(8,128)S(1)}, f32[64,9,3,64]{3,0,2,1:T(8,128)S(1)}, u32[]{:S(2)}, u32[]{:S(2)}) %collective-permute-start.12) | collective-permute-done | bytes 442400 | tf_op jit(solution)/shard_map/ppermute | solution.py:162
  243.1 2.1 sine_select_fusion
  245.4 3.0 %fusion.57 = f32[9,3,64,512]{3,2,1,0:T(8,128)S(1)} fusion(f32[64,9,3,64]{3,0,2,1:T(8,128)S(1)} %fusion.66, f32[512,256]{0,1:T(8,128)S(1)} %sine_select_fusion, s32[]{:T(128)S(6)} %select_n.187), kind=kOutput, calls=%fused_computation.127 | convolution fusion | flops 679477248 | bytes 4554756 | tf_op jit(solution)/shard_map/mfpz,xm->fpzx/dot_general | solution.py:163
  248.3 7.3 %collective-permute-done.13 = f32[64,9,3,64]{3,0,2,1:T(8,128)S(1)} collective-permute-done((f32[64,9,3,64]{3,0,2,1:T(8,128)S(1)}, f32[64,9,3,64]{3,0,2,1:T(8,128)S(1)}, u32[]{:S(2)}, u32[]{:S(2)}) %collective-permute-start.13) | collective-permute-done | bytes 442400 | tf_op jit(solution)/shard_map/ppermute | solution.py:162
  255.8 3.0 %fusion.55 = f32[9,3,64,512]{3,2,1,0:T(8,128)S(1)} fusion(f32[64,9,3,64]{3,0,2,1:T(8,128)S(1)} %collective-permute-done.12, f32[512,256]{0,1:T(8,128)S(1)} %sine_select_fusion, s32[]{:T(128)S(6)} %select_n.189), kind=kOutput, calls=%fused_computation.125 | convolution fusion | flops 679477248 | bytes 4554756 | tf_op jit(solution)/shard_map/mfpz,xm->fpzx/dot_general | solution.py:163
  258.8 3.0 %fusion.53 = f32[9,3,64,512]{3,2,1,0:T(8,128)S(1)} fusion(f32[64,9,3,64]{3,0,2,1:T(8,128)S(1)} %collective-permute-done.13, f32[512,256]{0,1:T(8,128)S(1)} %sine_select_fusion, s32[]{:T(128)S(6)} %select_n.191), kind=kOutput, calls=%fused_computation.123 | convolution fusion | flops 679477248 | bytes 4554756 | tf_op jit(solution)/shard_map/mfpz,xm->fpzx/dot_general | solution.py:163
  261.7 6.5 %collective-permute-done.14 = f32[64,9,3,64]{3,0,2,1:T(8,128)S(1)} collective-permute-done((f32[64,9,3,64]{3,0,2,1:T(8,128)S(1)}, f32[64,9,3,64]{3,0,2,1:T(8,128)S(1)}, u32[]{:S(2)}, u32[]{:S(2)}) %collective-permute-start.14) | collective-permute-done | bytes 442400 | tf_op jit(solution)/shard_map/ppermute | solution.py:162
  268.2 3.5 %add_add_fusion = f32[9,3,64,512]{3,2,1,0:T(8,128)S(1)} fusion(f32[9,3,64,512]{3,2,1,0:T(8,128)S(1)} %fusion.53, f32[9,3,64,512]{3,2,1,0:T(8,128)S(1)} %fusion.57, f32[9,3,64,512]{3,2,1,0:T(8,128)S(1)} %fusion.55, f32[64,9,3,64]{3,0,2,1:T(8,128)S(1)} %collective-permute-done.14, f32[512,256]{0,1:T(8,128)S(1)} %sine_select_fusion, s32[]{:T(128)S(6)} %select_n.193), kind=kOutput, calls=%fused_computation.2 | convolution fusion | flops 682131456 | bytes 15171588 | tf_op jit(solution)/shard_map/mfpz,xm->fpzx/dot_general | solution.py:163
  272.3 1.4 copy-done.2
  (71 shorter events, 5.2 us)
Async XLA Ops:
  7.2 9.0 %copy-start = (f32[3,3,64,512]{3,2,1,0:T(8,128)S(1)}, f32[3,3,64,512]{3,2,1,0:T(8,128)}, u32[]{:S(2)}) copy-start(f32[3,3,64,512]{3,2,1,0:T(8,128)} %param.4) | copy-start | bytes 3538948
  7.2 110.3 %reduce-scatter.2.cloned.1.call-start = ((), (), s32[]{:S(2)}) async-start(), calls=%async_computation.3 | async-start | bytes 4423680 | tf_op jit(solution)/shard_map/reduce_scatter | solution.py:123
  8.3 7.8 %collective-permute-start = (f32[3,3,1,512]{3,2,1,0:T(1,128)S(1)}, f32[3,3,1,512]{3,2,1,0:T(1,128)S(1)}, u32[]{:S(2)}, u32[]{:S(2)}) collective-permute-start(f32[3,3,1,512]{3,2,1,0:T(1,128)S(1)} %get-tuple-element.20), channel_id=1, source_target_pairs={{0,1},{1,2},{2,3},{3,4},{4,5},{5,6},{6,7},{7,0},{8,9},{9,10},{10,1... | collective-permute-start | bytes 55304 | tf_op jit(solution)/shard_map/ppermute | solution.py:24
  11.3 4.8 %collective-permute-start.1 = (f32[3,3,1,512]{3,2,1,0:T(1,128)S(1)}, f32[3,3,1,512]{3,2,1,0:T(1,128)S(1)}, u32[]{:S(2)}, u32[]{:S(2)}) collective-permute-start(f32[3,3,1,512]{3,2,1,0:T(1,128)S(1)} %get-tuple-element.21), channel_id=1, source_target_pairs={{1,0},{2,1},{3,2},{4,3},{5,4},{6,5},{7,6},{0,7},{9,8},{10,9},{11,1... | collective-permute-start | bytes 55304 | tf_op jit(solution)/shard_map/ppermute | solution.py:26
  16.3 8.1 %collective-permute-start.3 = (f32[3,3,66,1]{3,2,1,0:T(8,128)S(1)}, f32[3,3,66,1]{3,2,1,0:T(8,128)S(1)}, u32[]{:S(2)}, u32[]{:S(2)}) collective-permute-start(f32[3,3,66,1]{3,2,1,0:T(8,128)S(1)} %get-tuple-element.8), channel_id=1, source_target_pairs={{0,8},{8,16},{16,24},{24,0},{1,9},{9,17},{17,25},{25,1},{2,10},{10... | collective-permute-start | bytes 7136 | tf_op jit(solution)/shard_map/ppermute | solution.py:24
  16.4 9.3 %collective-permute-start.2 = (f32[3,3,66,1]{3,2,1,0:T(8,128)S(1)}, f32[3,3,66,1]{3,2,1,0:T(8,128)S(1)}, u32[]{:S(2)}, u32[]{:S(2)}) collective-permute-start(f32[3,3,66,1]{3,2,1,0:T(8,128)S(1)} %get-tuple-element.9), channel_id=1, source_target_pairs={{8,0},{16,8},{24,16},{0,24},{9,1},{17,9},{25,17},{1,25},{10,2},{18... | collective-permute-start | bytes 7136 | tf_op jit(solution)/shard_map/ppermute | solution.py:26
  26.9 0.7 copy-start.4
  27.9 8.7 %copy-start.3 = (f32[3]{0:T(128)S(1)}, f32[3]{0:T(128)}, u32[]{:S(2)}) copy-start(f32[3]{0:T(128)} %param.5) | copy-start | bytes 40
  28.0 6.7 %collective-permute-start.4 = (f32[3,3,1,512]{3,2,1,0:T(1,128)S(1)}, f32[3,3,1,512]{3,2,1,0:T(1,128)S(1)}, u32[]{:S(2)}, u32[]{:S(2)}) collective-permute-start(f32[3,3,1,512]{3,2,1,0:T(1,128)S(1)} %get-tuple-element.16), channel_id=1, source_target_pairs={{0,1},{1,2},{2,3},{3,4},{4,5},{5,6},{6,7},{7,0},{8,9},{9,10},{10,1... | collective-permute-start | bytes 55304 | tf_op jit(solution)/shard_map/ppermute | solution.py:24
  29.3 5.4 %collective-permute-start.5 = (f32[3,3,1,512]{3,2,1,0:T(1,128)S(1)}, f32[3,3,1,512]{3,2,1,0:T(1,128)S(1)}, u32[]{:S(2)}, u32[]{:S(2)}) collective-permute-start(f32[3,3,1,512]{3,2,1,0:T(1,128)S(1)} %get-tuple-element.17), channel_id=1, source_target_pairs={{1,0},{2,1},{3,2},{4,3},{5,4},{6,5},{7,6},{0,7},{9,8},{10,9},{11,1... | collective-permute-start | bytes 55304 | tf_op jit(solution)/shard_map/ppermute | solution.py:26
  34.8 8.1 %collective-permute-start.7 = (f32[3,3,66,1]{3,2,1,0:T(8,128)S(1)}, f32[3,3,66,1]{3,2,1,0:T(8,128)S(1)}, u32[]{:S(2)}, u32[]{:S(2)}) collective-permute-start(f32[3,3,66,1]{3,2,1,0:T(8,128)S(1)} %get-tuple-element.6), channel_id=1, source_target_pairs={{0,8},{8,16},{16,24},{24,0},{1,9},{9,17},{17,25},{25,1},{2,10},{10... | collective-permute-start | bytes 7136 | tf_op jit(solution)/shard_map/ppermute | solution.py:24
  35.0 9.2 %collective-permute-start.6 = (f32[3,3,66,1]{3,2,1,0:T(8,128)S(1)}, f32[3,3,66,1]{3,2,1,0:T(8,128)S(1)}, u32[]{:S(2)}, u32[]{:S(2)}) collective-permute-start(f32[3,3,66,1]{3,2,1,0:T(8,128)S(1)} %get-tuple-element.7), channel_id=1, source_target_pairs={{8,0},{16,8},{24,16},{0,24},{9,1},{17,9},{25,17},{1,25},{10,2},{18... | collective-permute-start | bytes 7136 | tf_op jit(solution)/shard_map/ppermute | solution.py:26
  46.1 6.5 %collective-permute-start.8 = (f32[3,3,1,512]{3,2,1,0:T(1,128)S(1)}, f32[3,3,1,512]{3,2,1,0:T(1,128)S(1)}, u32[]{:S(2)}, u32[]{:S(2)}) collective-permute-start(f32[3,3,1,512]{3,2,1,0:T(1,128)S(1)} %get-tuple-element.12), channel_id=1, source_target_pairs={{0,1},{1,2},{2,3},{3,4},{4,5},{5,6},{6,7},{7,0},{8,9},{9,10},{10,1... | collective-permute-start | bytes 55304 | tf_op jit(solution)/shard_map/ppermute | solution.py:24
  46.1 6.5 %collective-permute-start.9 = (f32[3,3,1,512]{3,2,1,0:T(1,128)S(1)}, f32[3,3,1,512]{3,2,1,0:T(1,128)S(1)}, u32[]{:S(2)}, u32[]{:S(2)}) collective-permute-start(f32[3,3,1,512]{3,2,1,0:T(1,128)S(1)} %get-tuple-element.13), channel_id=1, source_target_pairs={{1,0},{2,1},{3,2},{4,3},{5,4},{6,5},{7,6},{0,7},{9,8},{10,9},{11,1... | collective-permute-start | bytes 55304 | tf_op jit(solution)/shard_map/ppermute | solution.py:26
  52.8 7.4 %collective-permute-start.11 = (f32[3,3,66,1]{3,2,1,0:T(8,128)S(1)}, f32[3,3,66,1]{3,2,1,0:T(8,128)S(1)}, u32[]{:S(2)}, u32[]{:S(2)}) collective-permute-start(f32[3,3,66,1]{3,2,1,0:T(8,128)S(1)} %get-tuple-element.4), channel_id=1, source_target_pairs={{0,8},{8,16},{16,24},{24,0},{1,9},{9,17},{17,25},{25,1},{2,10},{10... | collective-permute-start | bytes 7136 | tf_op jit(solution)/shard_map/ppermute | solution.py:24
  52.8 9.6 %collective-permute-start.10 = (f32[3,3,66,1]{3,2,1,0:T(8,128)S(1)}, f32[3,3,66,1]{3,2,1,0:T(8,128)S(1)}, u32[]{:S(2)}, u32[]{:S(2)}) collective-permute-start(f32[3,3,66,1]{3,2,1,0:T(8,128)S(1)} %get-tuple-element.5), channel_id=1, source_target_pairs={{8,0},{16,8},{24,16},{0,24},{9,1},{17,9},{25,17},{1,25},{10,2},{18... | collective-permute-start | bytes 7136 | tf_op jit(solution)/shard_map/ppermute | solution.py:26
  64.2 1.0 copy-start.1
  119.6 6.9 %copy-start.5 = (s32[3,2]{0,1:T(2,128)S(1)}, s32[3,2]{0,1:T(2,128)}, u32[]{:S(2)}) copy-start(s32[3,2]{0,1:T(2,128)} %param.7) | copy-start | bytes 76
  120.8 20.0 %all-to-all-start = ((f32[8,216,64]{1,2,0:T(8,128)}), f32[8,216,64]{1,2,0:T(8,128)S(1)}, u32[]{:S(2)}, u32[]{:S(2)}) async-start(f32[8,216,64]{1,2,0:T(8,128)} %copy.20), calls=%async_computation.1 | async-start | bytes 1048576 | tf_op jit(solution)/shard_map/all_to_all | solution.py:134
  145.4 12.7 %all-to-all-start.1 = ((f32[8,32,216]{2,1,0:T(8,128)}), f32[8,32,216]{2,1,0:T(8,128)S(1)}, u32[]{:S(2)}, u32[]{:S(2)}) async-start(f32[8,32,216]{2,1,0:T(8,128)} %fusion.15), calls=%async_computation.2 | async-start | bytes 524288 | tf_op jit(solution)/shard_map/all_to_all | solution.py:139
  149.0 73.7 %all-gather.2.cloned.1.call-start = ((), (), s32[]{:S(2)}) async-start(), calls=%async_computation.4 | async-start | bytes 3981312 | tf_op jit(solution)/shard_map/all_gather | solution.py:153
  230.6 12.5 %collective-permute-start.12 = (f32[64,9,3,64]{3,0,2,1:T(8,128)S(1)}, f32[64,9,3,64]{3,0,2,1:T(8,128)S(1)}, u32[]{:S(2)}, u32[]{:S(2)}) collective-permute-start(f32[64,9,3,64]{3,0,2,1:T(8,128)S(1)} %fusion.66), channel_id=1, source_target_pairs={{0,8},{8,16},{16,24},{24,0},{1,9},{9,17},{17,25},{25,1},{2,10},{10... | collective-permute-start | bytes 1327112 | tf_op jit(solution)/shard_map/ppermute | solution.py:162
  243.1 12.5 %collective-permute-start.13 = (f32[64,9,3,64]{3,0,2,1:T(8,128)S(1)}, f32[64,9,3,64]{3,0,2,1:T(8,128)S(1)}, u32[]{:S(2)}, u32[]{:S(2)}) collective-permute-start(f32[64,9,3,64]{3,0,2,1:T(8,128)S(1)} %collective-permute-done.12), channel_id=1, source_target_pairs={{0,8},{8,16},{16,24},{24,0},{1,9},{9,17},{17,25},{25,1},{2,10},{10... | collective-permute-start | bytes 1327112 | tf_op jit(solution)/shard_map/ppermute | solution.py:162
  255.6 12.7 %collective-permute-start.14 = (f32[64,9,3,64]{3,0,2,1:T(8,128)S(1)}, f32[64,9,3,64]{3,0,2,1:T(8,128)S(1)}, u32[]{:S(2)}, u32[]{:S(2)}) collective-permute-start(f32[64,9,3,64]{3,0,2,1:T(8,128)S(1)} %collective-permute-done.13), channel_id=1, source_target_pairs={{0,8},{8,16},{16,24},{24,0},{1,9},{9,17},{17,25},{25,1},{2,10},{10... | collective-permute-start | bytes 1327112 | tf_op jit(solution)/shard_map/ppermute | solution.py:162
  272.3 1.4 copy-start.2
Sparse Core Ops, SparseCore 0:
  75.2 42.1 reduce-scatter.1
  160.0 62.6 all-gather.1
